TPU v7x, 32 devices: a whole 2x2x4 slice. The times are simulated.
32 devices in a mesh: tm: 8 (over y, x, core), space: 4 (over z).
Axes of the slice: x: 2, y: 2, z: 4, core: 2. Of those that a mesh axis runs over, the one named last changes fastest.
Arguments:
- guess: float32 [32, 128, 4096], P('tm', 'space'), may hold values from -6 to 6
- forcing: float32 [32, 128, 4096], P('tm', 'space'), may hold values from -4 to 4
- initial: float32 [128, 4096], P('space'), may hold values from -6 to 6
- courant_rows: float32 [128, 4096], P('space'), may hold values from -0.12 to 0.12
- courant_cols: float32 [128, 4096], P('space'), may hold values from -0.12 to 0.12
- diffusion: float32 [128, 4096], P('space'), may hold values from 0.03 to 0.06
Outputs:
- states: float32 [32, 128, 4096], P('tm', 'space')
All inputs are finite; a program needn't handle non-finite values.
Results may differ from a plain program's by a relative error of at most 0.00002.
Values sent between devices are 32-bit elements; how exact they have to be, the bound alone decides.
A program may use at most 64 MiB of HBM per device.

v0:
```python
import jax
import jax.numpy as jnp
from jax import lax
from jax.sharding import PartitionSpec as P


def padded(value, sides, width):
    for axis, dim in sides:
        count, length = (lax.axis_size(axis), value.shape[dim])
        up = [(i, (i + 1) % count) for i in range(count - 1)]
        down = [(j, i) for i, j in up]
        last = lax.slice_in_dim(value, length - width, length, axis=dim)
        leading = lax.slice_in_dim(value, 0, width, axis=dim)
        before = lax.ppermute(last, axis, up)
        after = lax.ppermute(leading, axis, down)
        value = jnp.concatenate([before, value, after], axis=dim)
    return value


def passed_along(value, axis, steps):
    count = lax.axis_size(axis)
    leading, last = (max(0, -steps), min(count, count - steps))
    return lax.ppermute(value, axis, [(source, source + steps) for source in range(leading, last)])


def local_step(extended, rate_rows, rate_cols, spread):
    field = extended[1:-1]
    upper = extended[:-2]
    lower = extended[2:]
    left = jnp.roll(field, 1, axis=1)
    right = jnp.roll(field, -1, axis=1)
    advect = jnp.maximum(rate_rows, 0.0) * (field - upper) + jnp.minimum(rate_rows, 0.0) * (
        lower - field
    )
    advect = (
        advect
        + jnp.maximum(rate_cols, 0.0) * (field - left)
        + jnp.minimum(rate_cols, 0.0) * (right - field)
    )
    laplace = upper + lower + left + right - 4.0 * field
    return field - advect + spread * laplace


def advance(field, rate_rows, rate_cols, spread):
    extended = padded(field, (("space", 0),), 1)
    return local_step(extended, rate_rows, rate_cols, spread)


def leap_apply(incoming, coeff_pad, widest, depth, row_first, row_total):
    extended = padded(incoming, (("space", 0),), depth)
    height = incoming.shape[0]
    window = coeff_pad[:, widest - depth : widest + depth + height]
    for inner in range(depth):
        span = height + 2 * (depth - inner) - 2
        sliced = window[:, inner + 1 : inner + 1 + span]
        result = local_step(extended, 2.0 * sliced[0], 2.0 * sliced[1], 2.0 * sliced[2])
        global_rows = row_first - (depth - inner - 1) + jnp.arange(span)
        inside = (global_rows >= 0) & (global_rows < row_total)
        extended = jnp.where(inside[:, None], result, 0.0)
    return extended


def on_device(guess, forcing, initial, courant_rows, courant_cols, diffusion):
    steps_dev = guess.shape[0]
    height = guess.shape[1]
    owners = lax.axis_size("tm")
    is_first = lax.axis_index("tm") == 0
    row_first = lax.axis_index("space") * height
    row_total = height * lax.axis_size("space")
    previous = passed_along(guess[steps_dev - 1], "tm", 1)
    current = jnp.where(is_first, initial, previous)
    for inner in range(steps_dev):
        current = advance(current, courant_rows, courant_cols, diffusion) + forcing[inner]
    residual = current - guess[steps_dev - 1]
    distances = [1 << level for level in range(owners.bit_length()) if 1 << level < owners]
    widest = steps_dev // 2 * distances[-1]
    stacked = jnp.stack([courant_rows, courant_cols, diffusion])
    coeff_pad = padded(stacked, (("space", 1),), widest)
    correction = residual
    for distance in distances:
        incoming = passed_along(correction, "tm", distance)
        correction = correction + leap_apply(
            incoming, coeff_pad, widest, steps_dev // 2 * distance, row_first, row_total
        )
    corrected = guess[steps_dev - 1] + correction
    handed = passed_along(corrected, "tm", 1)
    current = jnp.where(is_first, initial, handed)
    outputs = []
    for inner in range(steps_dev - 1):
        current = advance(current, courant_rows, courant_cols, diffusion) + forcing[inner]
        outputs.append(current)
    outputs.append(corrected)
    return jnp.stack(outputs)


def solution(mesh):
    return jax.shard_map(
        on_device,
        mesh=mesh,
        in_specs=(
            P("tm", "space", None),
            P("tm", "space", None),
            P("space", None),
            P("space", None),
            P("space", None),
            P("space", None),
        ),
        out_specs=P("tm", "space", None),
        check_vma=False,
    )
```

profile of v0, /device:TPU:4, one launch (start us, length us, event | category | flops | bytes accessed | tf_op | source)
XLA Modules:
  0.0 178.7 jit_solution(3220405049372623573)
XLA Ops:
  3.1 2.1 %pad_maximum_fusion.67 = (f32[3,8,4096]{2,1,0:T(8,128)}, f32[3,8,4096]{2,1,0:T(8,128)}) fusion(f32[1,32,4096]{2,1,0:T(8,128)} %bitcast.339, f32[1,32,4096]{2,1,0:T(8,128)} %bitcast.341, f32[1,32,4096]{2,1,0:T(8,128)} %bitcast.343), kind=kLoop, calls=%fused_computation.332 | loop fusion | flops 393216 | bytes 2359296 | tf_op jit(solution)/shard_map/slice | solution.py:12
  5.2 4.4 %collective-permute-start.12 = (f32[3,8,4096]{2,1,0:T(8,128)}, f32[3,8,4096]{2,1,0:T(8,128)}, u32[]{:S(2)}, u32[]{:S(2)}) collective-permute-start(f32[3,8,4096]{2,1,0:T(8,128)} %get-tuple-element.5), channel_id=1, source_target_pairs={{0,1},{1,2},{2,3},{4,5},{5,6},{6,7},{8,9},{9,10},{10,11},{12,13},{... | collective-permute-start | bytes 1179656 | tf_op jit(solution)/shard_map/ppermute | solution.py:14
  12.8 3.5 %collective-permute-start.1 = (f32[1,4096]{1,0:T(1,128)S(1)}, f32[1,4096]{1,0:T(1,128)S(1)}, u32[]{:S(2)}, u32[]{:S(2)}) collective-permute-start(f32[1,4096]{1,0:T(1,128)S(1)} %get-tuple-element.105), channel_id=1, source_target_pairs={{0,1},{1,2},{2,3},{4,5},{5,6},{6,7},{8,9},{9,10},{10,11},{12,13},{... | collective-permute-start | bytes 49160 | tf_op jit(solution)/shard_map/ppermute | solution.py:14
  18.3 5.4 %collective-permute-done.2 = f32[1,4096]{1,0:T(1,128)S(1)} collective-permute-done((f32[1,4096]{1,0:T(1,128)S(1)}, f32[1,4096]{1,0:T(1,128)S(1)}, u32[]{:S(2)}, u32[]{:S(2)}) %collective-permute-start.2) | collective-permute-done | bytes 16416 | tf_op jit(solution)/shard_map/ppermute | solution.py:15
  24.5 2.7 %collective-permute-start.3 = (f32[1,4096]{1,0:T(1,128)S(1)}, f32[1,4096]{1,0:T(1,128)S(1)}, u32[]{:S(2)}, u32[]{:S(2)}) collective-permute-start(f32[1,4096]{1,0:T(1,128)S(1)} %get-tuple-element.99), channel_id=1, source_target_pairs={{0,1},{1,2},{2,3},{4,5},{5,6},{6,7},{8,9},{9,10},{10,11},{12,13},{... | collective-permute-start | bytes 49160 | tf_op jit(solution)/shard_map/ppermute | solution.py:14
  28.7 4.2 %collective-permute-done.4 = f32[1,4096]{1,0:T(1,128)S(1)} collective-permute-done((f32[1,4096]{1,0:T(1,128)S(1)}, f32[1,4096]{1,0:T(1,128)S(1)}, u32[]{:S(2)}, u32[]{:S(2)}) %collective-permute-start.4) | collective-permute-done | bytes 16416 | tf_op jit(solution)/shard_map/ppermute | solution.py:15
  33.7 3.5 %collective-permute-start.5 = (f32[1,4096]{1,0:T(1,128)S(1)}, f32[1,4096]{1,0:T(1,128)S(1)}, u32[]{:S(2)}, u32[]{:S(2)}) collective-permute-start(f32[1,4096]{1,0:T(1,128)S(1)} %get-tuple-element.93), channel_id=1, source_target_pairs={{0,1},{1,2},{2,3},{4,5},{5,6},{6,7},{8,9},{9,10},{10,11},{12,13},{... | collective-permute-start | bytes 49160 | tf_op jit(solution)/shard_map/ppermute | solution.py:14
  38.6 4.2 %collective-permute-done.6 = f32[1,4096]{1,0:T(1,128)S(1)} collective-permute-done((f32[1,4096]{1,0:T(1,128)S(1)}, f32[1,4096]{1,0:T(1,128)S(1)}, u32[]{:S(2)}, u32[]{:S(2)}) %collective-permute-start.6) | collective-permute-done | bytes 16416 | tf_op jit(solution)/shard_map/ppermute | solution.py:15
  47.0 4.2 %collective-permute-done.8 = f32[1,4096]{1,0:T(1,128)S(1)} collective-permute-done((f32[1,4096]{1,0:T(1,128)S(1)}, f32[1,4096]{1,0:T(1,128)S(1)}, u32[]{:S(2)}, u32[]{:S(2)}) %collective-permute-start.8) | collective-permute-done | bytes 16416 | tf_op jit(solution)/shard_map/ppermute | solution.py:15
  52.9 1.9 %collective-permute-start.9 = (f32[32,4096]{1,0:T(8,128)S(1)}, f32[32,4096]{1,0:T(8,128)S(1)}, u32[]{:S(2)}, u32[]{:S(2)}) collective-permute-start(f32[32,4096]{1,0:T(8,128)S(1)} %fusion.139), channel_id=1, source_target_pairs={{0,4},{4,8},{8,12},{12,16},{16,20},{20,24},{24,28},{1,5},{5,9},{9,... | collective-permute-start | bytes 1572872 | tf_op jit(solution)/shard_map/ppermute | solution.py:23
  56.1 8.2 %collective-permute-done.9 = f32[32,4096]{1,0:T(8,128)S(1)} collective-permute-done((f32[32,4096]{1,0:T(8,128)S(1)}, f32[32,4096]{1,0:T(8,128)S(1)}, u32[]{:S(2)}, u32[]{:S(2)}) %collective-permute-start.9) | collective-permute-done | bytes 524320 | tf_op jit(solution)/shard_map/ppermute | solution.py:23
  64.3 1.9 %collective-permute-start.10 = (f32[2,4096]{1,0:T(2,128)S(1)}, f32[2,4096]{1,0:T(2,128)S(1)}, u32[]{:S(2)}, u32[]{:S(2)}) collective-permute-start(f32[2,4096]{1,0:T(2,128)S(1)} %get-tuple-element.81), channel_id=1, source_target_pairs={{0,1},{1,2},{2,3},{4,5},{5,6},{6,7},{8,9},{9,10},{10,11},{12,13},{... | collective-permute-start | bytes 98312 | tf_op jit(solution)/shard_map/ppermute | solution.py:14
  67.8 4.2 %collective-permute-done.11 = f32[2,4096]{1,0:T(2,128)S(1)} collective-permute-done((f32[2,4096]{1,0:T(2,128)S(1)}, f32[2,4096]{1,0:T(2,128)S(1)}, u32[]{:S(2)}, u32[]{:S(2)}) %collective-permute-start.11) | collective-permute-done | bytes 32800 | tf_op jit(solution)/shard_map/ppermute | solution.py:15
  76.8 10.6 %collective-permute-done.14 = f32[32,4096]{1,0:T(8,128)} collective-permute-done((f32[32,4096]{1,0:T(8,128)}, f32[32,4096]{1,0:T(8,128)}, u32[]{:S(2)}, u32[]{:S(2)}) %collective-permute-start.14) | collective-permute-done | bytes 524320 | tf_op jit(solution)/shard_map/ppermute | solution.py:23
  88.4 2.4 %collective-permute-start.15 = (f32[4,4096]{1,0:T(4,128)S(1)}, f32[4,4096]{1,0:T(4,128)S(1)}, u32[]{:S(2)}, u32[]{:S(2)}) collective-permute-start(f32[4,4096]{1,0:T(4,128)S(1)} %get-tuple-element.79), channel_id=1, source_target_pairs={{0,1},{1,2},{2,3},{4,5},{5,6},{6,7},{8,9},{9,10},{10,11},{12,13},{... | collective-permute-start | bytes 196616 | tf_op jit(solution)/shard_map/ppermute | solution.py:14
  92.7 4.3 %collective-permute-done.16 = f32[4,4096]{1,0:T(4,128)S(1)} collective-permute-done((f32[4,4096]{1,0:T(4,128)S(1)}, f32[4,4096]{1,0:T(4,128)S(1)}, u32[]{:S(2)}, u32[]{:S(2)}) %collective-permute-start.16) | collective-permute-done | bytes 65568 | tf_op jit(solution)/shard_map/ppermute | solution.py:15
  103.3 2.4 %select_add_fusion = f32[32,4096]{1,0:T(8,128)} fusion(f32[32,4096]{1,0:T(8,128)} %select_add_fusion.1, f32[32,1]{1,0:T(8,128)S(1)} %get-tuple-element.40, f32[32,4095]{1,0:T(8,128)S(1)} %get-tuple-element.42, f32[32,4095]{1,0:T(8,128)S(1)} %get-tuple-element.41, f32[32,1]{1,0:T(8,128)S(1)} %get-tuple-element.39, f32[34,4096]{1,0:T(8,128)S(1)} %fusion.70, ...), kind=kLoop, calls=%fused_computation.323 | loop fusion | flops 3932160 | bytes 5242912 | tf_op jit(solution)/shard_map/add | solution.py:82
  108.2 8.9 %collective-permute-done.17 = f32[32,4096]{1,0:T(8,128)} collective-permute-done((f32[32,4096]{1,0:T(8,128)}, f32[32,4096]{1,0:T(8,128)}, u32[]{:S(2)}, u32[]{:S(2)}) %collective-permute-start.17) | collective-permute-done | bytes 524320 | tf_op jit(solution)/shard_map/ppermute | solution.py:23
  124.7 3.7 %collective-permute-done.19 = f32[8,4096]{1,0:T(8,128)S(1)} collective-permute-done((f32[8,4096]{1,0:T(8,128)}, f32[8,4096]{1,0:T(8,128)S(1)}, u32[]{:S(2)}, u32[]{:S(2)}) %collective-permute-start.19) | collective-permute-done | bytes 131104 | tf_op jit(solution)/shard_map/ppermute | solution.py:15
  140.6 2.1 %collective-permute-start.20 = (f32[32,4096]{1,0:T(8,128)S(1)}, f32[32,4096]{1,0:T(8,128)S(1)}, u32[]{:S(2)}, u32[]{:S(2)}) collective-permute-start(f32[32,4096]{1,0:T(8,128)S(1)} %add_add_fusion), channel_id=1, source_target_pairs={{0,4},{4,8},{8,12},{12,16},{16,20},{20,24},{24,28},{1,5},{5,9},{9,... | collective-permute-start | bytes 1572872 | tf_op jit(solution)/shard_map/ppermute | solution.py:23
  142.6 9.5 %collective-permute-done.20 = f32[32,4096]{1,0:T(8,128)S(1)} collective-permute-done((f32[32,4096]{1,0:T(8,128)S(1)}, f32[32,4096]{1,0:T(8,128)S(1)}, u32[]{:S(2)}, u32[]{:S(2)}) %collective-permute-start.20) | collective-permute-done | bytes 524320 | tf_op jit(solution)/shard_map/ppermute | solution.py:23
  155.8 4.2 %collective-permute-done.22 = f32[1,4096]{1,0:T(1,128)S(1)} collective-permute-done((f32[1,4096]{1,0:T(1,128)S(1)}, f32[1,4096]{1,0:T(1,128)S(1)}, u32[]{:S(2)}, u32[]{:S(2)}) %collective-permute-start.22) | collective-permute-done | bytes 16416 | tf_op jit(solution)/shard_map/ppermute | solution.py:15
  164.1 4.2 %collective-permute-done.24 = f32[1,4096]{1,0:T(1,128)S(1)} collective-permute-done((f32[1,4096]{1,0:T(1,128)S(1)}, f32[1,4096]{1,0:T(1,128)S(1)}, u32[]{:S(2)}, u32[]{:S(2)}) %collective-permute-start.24) | collective-permute-done | bytes 16416 | tf_op jit(solution)/shard_map/ppermute | solution.py:15
  172.5 4.2 %collective-permute-done.26 = f32[1,4096]{1,0:T(1,128)S(1)} collective-permute-done((f32[1,4096]{1,0:T(1,128)S(1)}, f32[1,4096]{1,0:T(1,128)S(1)}, u32[]{:S(2)}, u32[]{:S(2)}) %collective-permute-start.26) | collective-permute-done | bytes 16416 | tf_op jit(solution)/shard_map/ppermute | solution.py:15
  (148 shorter events, 71.2 us)
Async XLA Ops:
  1.1 11.4 %collective-permute-start = (f32[32,4096]{1,0:T(8,128)S(1)}, f32[32,4096]{1,0:T(8,128)S(1)}, u32[]{:S(2)}, u32[]{:S(2)}) collective-permute-start(f32[32,4096]{1,0:T(8,128)S(1)} %slice_bitcast_fusion), channel_id=1, source_target_pairs={{0,4},{4,8},{8,12},{12,16},{16,20},{20,24},{24,28},{1,5},{5,9},{9,... | collective-permute-start | bytes 1572872 | tf_op jit(solution)/shard_map/ppermute | solution.py:23
  5.2 49.6 %collective-permute-start.12 = (f32[3,8,4096]{2,1,0:T(8,128)}, f32[3,8,4096]{2,1,0:T(8,128)}, u32[]{:S(2)}, u32[]{:S(2)}) collective-permute-start(f32[3,8,4096]{2,1,0:T(8,128)} %get-tuple-element.5), channel_id=1, source_target_pairs={{0,1},{1,2},{2,3},{4,5},{5,6},{6,7},{8,9},{9,10},{10,11},{12,13},{... | collective-permute-start | bytes 1179656 | tf_op jit(solution)/shard_map/ppermute | solution.py:14
  9.6 45.2 %collective-permute-start.13 = (f32[3,8,4096]{2,1,0:T(8,128)}, f32[3,8,4096]{2,1,0:T(8,128)}, u32[]{:S(2)}, u32[]{:S(2)}) collective-permute-start(f32[3,8,4096]{2,1,0:T(8,128)} %get-tuple-element.6), channel_id=1, source_target_pairs={{1,0},{2,1},{3,2},{5,4},{6,5},{7,6},{9,8},{10,9},{11,10},{13,12},{... | collective-permute-start | bytes 1179656 | tf_op jit(solution)/shard_map/ppermute | solution.py:15
  12.8 5.4 %collective-permute-start.1 = (f32[1,4096]{1,0:T(1,128)S(1)}, f32[1,4096]{1,0:T(1,128)S(1)}, u32[]{:S(2)}, u32[]{:S(2)}) collective-permute-start(f32[1,4096]{1,0:T(1,128)S(1)} %get-tuple-element.105), channel_id=1, source_target_pairs={{0,1},{1,2},{2,3},{4,5},{5,6},{6,7},{8,9},{9,10},{10,11},{12,13},{... | collective-permute-start | bytes 49160 | tf_op jit(solution)/shard_map/ppermute | solution.py:14
  16.3 7.3 %collective-permute-start.2 = (f32[1,4096]{1,0:T(1,128)S(1)}, f32[1,4096]{1,0:T(1,128)S(1)}, u32[]{:S(2)}, u32[]{:S(2)}) collective-permute-start(f32[1,4096]{1,0:T(1,128)S(1)} %get-tuple-element.106), channel_id=1, source_target_pairs={{1,0},{2,1},{3,2},{5,4},{6,5},{7,6},{9,8},{10,9},{11,10},{13,12},{... | collective-permute-start | bytes 49160 | tf_op jit(solution)/shard_map/ppermute | solution.py:15
  24.5 4.2 %collective-permute-start.3 = (f32[1,4096]{1,0:T(1,128)S(1)}, f32[1,4096]{1,0:T(1,128)S(1)}, u32[]{:S(2)}, u32[]{:S(2)}) collective-permute-start(f32[1,4096]{1,0:T(1,128)S(1)} %get-tuple-element.99), channel_id=1, source_target_pairs={{0,1},{1,2},{2,3},{4,5},{5,6},{6,7},{8,9},{9,10},{10,11},{12,13},{... | collective-permute-start | bytes 49160 | tf_op jit(solution)/shard_map/ppermute | solution.py:14
  27.3 5.6 %collective-permute-start.4 = (f32[1,4096]{1,0:T(1,128)S(1)}, f32[1,4096]{1,0:T(1,128)S(1)}, u32[]{:S(2)}, u32[]{:S(2)}) collective-permute-start(f32[1,4096]{1,0:T(1,128)S(1)} %get-tuple-element.100), channel_id=1, source_target_pairs={{1,0},{2,1},{3,2},{5,4},{6,5},{7,6},{9,8},{10,9},{11,10},{13,12},{... | collective-permute-start | bytes 49160 | tf_op jit(solution)/shard_map/ppermute | solution.py:15
  33.7 4.9 %collective-permute-start.5 = (f32[1,4096]{1,0:T(1,128)S(1)}, f32[1,4096]{1,0:T(1,128)S(1)}, u32[]{:S(2)}, u32[]{:S(2)}) collective-permute-start(f32[1,4096]{1,0:T(1,128)S(1)} %get-tuple-element.93), channel_id=1, source_target_pairs={{0,1},{1,2},{2,3},{4,5},{5,6},{6,7},{8,9},{9,10},{10,11},{12,13},{... | collective-permute-start | bytes 49160 | tf_op jit(solution)/shard_map/ppermute | solution.py:14
  37.2 5.6 %collective-permute-start.6 = (f32[1,4096]{1,0:T(1,128)S(1)}, f32[1,4096]{1,0:T(1,128)S(1)}, u32[]{:S(2)}, u32[]{:S(2)}) collective-permute-start(f32[1,4096]{1,0:T(1,128)S(1)} %get-tuple-element.94), channel_id=1, source_target_pairs={{1,0},{2,1},{3,2},{5,4},{6,5},{7,6},{9,8},{10,9},{11,10},{13,12},{... | collective-permute-start | bytes 49160 | tf_op jit(solution)/shard_map/ppermute | solution.py:15
  43.6 3.4 %collective-permute-start.7 = (f32[1,4096]{1,0:T(1,128)S(1)}, f32[1,4096]{1,0:T(1,128)S(1)}, u32[]{:S(2)}, u32[]{:S(2)}) collective-permute-start(f32[1,4096]{1,0:T(1,128)S(1)} %get-tuple-element.87), channel_id=1, source_target_pairs={{0,1},{1,2},{2,3},{4,5},{5,6},{6,7},{8,9},{9,10},{10,11},{12,13},{... | collective-permute-start | bytes 49160 | tf_op jit(solution)/shard_map/ppermute | solution.py:14
  45.5 5.6 %collective-permute-start.8 = (f32[1,4096]{1,0:T(1,128)S(1)}, f32[1,4096]{1,0:T(1,128)S(1)}, u32[]{:S(2)}, u32[]{:S(2)}) collective-permute-start(f32[1,4096]{1,0:T(1,128)S(1)} %get-tuple-element.88), channel_id=1, source_target_pairs={{1,0},{2,1},{3,2},{5,4},{6,5},{7,6},{9,8},{10,9},{11,10},{13,12},{... | collective-permute-start | bytes 49160 | tf_op jit(solution)/shard_map/ppermute | solution.py:15
  52.9 11.4 %collective-permute-start.9 = (f32[32,4096]{1,0:T(8,128)S(1)}, f32[32,4096]{1,0:T(8,128)S(1)}, u32[]{:S(2)}, u32[]{:S(2)}) collective-permute-start(f32[32,4096]{1,0:T(8,128)S(1)} %fusion.139), channel_id=1, source_target_pairs={{0,4},{4,8},{8,12},{12,16},{16,20},{20,24},{24,28},{1,5},{5,9},{9,... | collective-permute-start | bytes 1572872 | tf_op jit(solution)/shard_map/ppermute | solution.py:23
  64.3 3.5 %collective-permute-start.10 = (f32[2,4096]{1,0:T(2,128)S(1)}, f32[2,4096]{1,0:T(2,128)S(1)}, u32[]{:S(2)}, u32[]{:S(2)}) collective-permute-start(f32[2,4096]{1,0:T(2,128)S(1)} %get-tuple-element.81), channel_id=1, source_target_pairs={{0,1},{1,2},{2,3},{4,5},{5,6},{6,7},{8,9},{9,10},{10,11},{12,13},{... | collective-permute-start | bytes 98312 | tf_op jit(solution)/shard_map/ppermute | solution.py:14
  66.2 5.8 %collective-permute-start.11 = (f32[2,4096]{1,0:T(2,128)S(1)}, f32[2,4096]{1,0:T(2,128)S(1)}, u32[]{:S(2)}, u32[]{:S(2)}) collective-permute-start(f32[2,4096]{1,0:T(2,128)S(1)} %get-tuple-element.82), channel_id=1, source_target_pairs={{1,0},{2,1},{3,2},{5,4},{6,5},{7,6},{9,8},{10,9},{11,10},{13,12},{... | collective-permute-start | bytes 98312 | tf_op jit(solution)/shard_map/ppermute | solution.py:15
  74.9 12.5 %collective-permute-start.14 = (f32[32,4096]{1,0:T(8,128)}, f32[32,4096]{1,0:T(8,128)}, u32[]{:S(2)}, u32[]{:S(2)}) collective-permute-start(f32[32,4096]{1,0:T(8,128)} %select_add_fusion.1), channel_id=1, source_target_pairs={{0,8},{4,12},{8,16},{12,20},{16,24},{20,28},{1,9},{5,13},{9,17},{1... | collective-permute-start | bytes 1572872 | tf_op jit(solution)/shard_map/ppermute | solution.py:23
  88.4 4.3 %collective-permute-start.15 = (f32[4,4096]{1,0:T(4,128)S(1)}, f32[4,4096]{1,0:T(4,128)S(1)}, u32[]{:S(2)}, u32[]{:S(2)}) collective-permute-start(f32[4,4096]{1,0:T(4,128)S(1)} %get-tuple-element.79), channel_id=1, source_target_pairs={{0,1},{1,2},{2,3},{4,5},{5,6},{6,7},{8,9},{9,10},{10,11},{12,13},{... | collective-permute-start | bytes 196616 | tf_op jit(solution)/shard_map/ppermute | solution.py:14
  90.9 6.2 %collective-permute-start.16 = (f32[4,4096]{1,0:T(4,128)S(1)}, f32[4,4096]{1,0:T(4,128)S(1)}, u32[]{:S(2)}, u32[]{:S(2)}) collective-permute-start(f32[4,4096]{1,0:T(4,128)S(1)} %get-tuple-element.80), channel_id=1, source_target_pairs={{1,0},{2,1},{3,2},{5,4},{6,5},{7,6},{9,8},{10,9},{11,10},{13,12},{... | collective-permute-start | bytes 196616 | tf_op jit(solution)/shard_map/ppermute | solution.py:15
  105.8 11.4 %collective-permute-start.17 = (f32[32,4096]{1,0:T(8,128)}, f32[32,4096]{1,0:T(8,128)}, u32[]{:S(2)}, u32[]{:S(2)}) collective-permute-start(f32[32,4096]{1,0:T(8,128)} %select_add_fusion), channel_id=1, source_target_pairs={{0,16},{4,20},{8,24},{12,28},{1,17},{5,21},{9,25},{13,29},{2,18},{... | collective-permute-start | bytes 1572872 | tf_op jit(solution)/shard_map/ppermute | solution.py:23
  118.9 4.7 %collective-permute-start.18 = (f32[8,4096]{1,0:T(8,128)}, f32[8,4096]{1,0:T(8,128)S(1)}, u32[]{:S(2)}, u32[]{:S(2)}) collective-permute-start(f32[8,4096]{1,0:T(8,128)} %get-tuple-element.78), channel_id=1, source_target_pairs={{0,1},{1,2},{2,3},{4,5},{5,6},{6,7},{8,9},{9,10},{10,11},{12,13},{... | collective-permute-start | bytes 393224 | tf_op jit(solution)/shard_map/ppermute | solution.py:14
  121.3 7.1 %collective-permute-start.19 = (f32[8,4096]{1,0:T(8,128)}, f32[8,4096]{1,0:T(8,128)S(1)}, u32[]{:S(2)}, u32[]{:S(2)}) collective-permute-start(f32[8,4096]{1,0:T(8,128)} %get-tuple-element.77), channel_id=1, source_target_pairs={{1,0},{2,1},{3,2},{5,4},{6,5},{7,6},{9,8},{10,9},{11,10},{13,12},{... | collective-permute-start | bytes 393224 | tf_op jit(solution)/shard_map/ppermute | solution.py:15
  140.6 11.5 %collective-permute-start.20 = (f32[32,4096]{1,0:T(8,128)S(1)}, f32[32,4096]{1,0:T(8,128)S(1)}, u32[]{:S(2)}, u32[]{:S(2)}) collective-permute-start(f32[32,4096]{1,0:T(8,128)S(1)} %add_add_fusion), channel_id=1, source_target_pairs={{0,4},{4,8},{8,12},{12,16},{16,20},{20,24},{24,28},{1,5},{5,9},{9,... | collective-permute-start | bytes 1572872 | tf_op jit(solution)/shard_map/ppermute | solution.py:23
  154.3 5.6 %collective-permute-start.22 = (f32[1,4096]{1,0:T(1,128)S(1)}, f32[1,4096]{1,0:T(1,128)S(1)}, u32[]{:S(2)}, u32[]{:S(2)}) collective-permute-start(f32[1,4096]{1,0:T(1,128)S(1)} %get-tuple-element.76), channel_id=1, source_target_pairs={{1,0},{2,1},{3,2},{5,4},{6,5},{7,6},{9,8},{10,9},{11,10},{13,12},{... | collective-permute-start | bytes 49160 | tf_op jit(solution)/shard_map/ppermute | solution.py:15
  162.7 5.6 %collective-permute-start.24 = (f32[1,4096]{1,0:T(1,128)S(1)}, f32[1,4096]{1,0:T(1,128)S(1)}, u32[]{:S(2)}, u32[]{:S(2)}) collective-permute-start(f32[1,4096]{1,0:T(1,128)S(1)} %get-tuple-element.70), channel_id=1, source_target_pairs={{1,0},{2,1},{3,2},{5,4},{6,5},{7,6},{9,8},{10,9},{11,10},{13,12},{... | collective-permute-start | bytes 49160 | tf_op jit(solution)/shard_map/ppermute | solution.py:15
  171.0 5.6 %collective-permute-start.26 = (f32[1,4096]{1,0:T(1,128)S(1)}, f32[1,4096]{1,0:T(1,128)S(1)}, u32[]{:S(2)}, u32[]{:S(2)}) collective-permute-start(f32[1,4096]{1,0:T(1,128)S(1)} %get-tuple-element.64), channel_id=1, source_target_pairs={{1,0},{2,1},{3,2},{5,4},{6,5},{7,6},{9,8},{10,9},{11,10},{13,12},{... | collective-permute-start | bytes 49160 | tf_op jit(solution)/shard_map/ppermute | solution.py:15
  (16 other events, 138.1 us)
where the time goes:
time: 180 us; the launch traced here: 179 us
  waiting for transfers between devices  84.1 us (47%)
  starting transfers between devices  51.5 us (29%)
  other arithmetic  29.1 us (16%)
  local copies, waits for them, and re-layouts  13.5 us (8%)
    ppermute x11, waiting for transfers between devices, padded(): after = lax.ppermute(leading, axis, down)  42.8 us
    ppermute x5, waiting for transfers between devices, passed_along(): lax.ppermute(value, axis, [(source, source + steps) for source in range(l...  38.8 us
    ppermute x11, starting transfers between devices, padded(): before = lax.ppermute(last, axis, up)  28 us
    ppermute x11, starting transfers between devices, padded(): after = lax.ppermute(leading, axis, down)  14.4 us
    select_n x11, other arithmetic, leap_apply(): extended = jnp.where(inside[:, None], result, 0.0)  10.5 us
    ppermute x5, starting transfers between devices, passed_along(): lax.ppermute(value, axis, [(source, source + steps) for source in range(l...  9.08 us
    slice x40, local copies, waits for them, and re-layouts, local_step(): left = jnp.roll(field, 1, axis=1)  6.24 us
    add x2, other arithmetic, on_device(): correction + leap_apply(incoming, coeff_pad, widest, steps_dev // 2 * dis...  3.82 us
  transfers between devices with their start and end apart: 27, of which 25 were waited for; matrix products, arithmetic and copies ran while one was open for 6% of the time, Pallas kernels for 0%

commit v1 on v0

v1 whole, which is shorter than its diff:
```python
import functools

import jax
import jax.numpy as jnp
from jax import lax
from jax.experimental import pallas as pl
from jax.experimental.pallas import tpu as pltpu
from jax.sharding import PartitionSpec as P

TILE = 8
LANES = 128
MESH = pl.DeviceIdType.MESH


def packing(depth):
    items = [(("f", j), depth - 1 - j) for j in range(depth - 1)]
    items += [(("c", j), depth - 1) for j in range(3)]
    items = sorted(items, key=lambda item: -item[1])
    used, placed = [], []
    for source, rows in items:
        for tile in range(len(used) + 1):
            if tile == len(used):
                used.append(0)
            if used[tile] + rows <= TILE:
                placed.append((source, rows, tile, used[tile]))
                used[tile] += rows
                break
    return placed, len(used)


def rolled(value, shift, axis):
    shift = shift % value.shape[axis]
    return pltpu.roll(value, shift, axis) if shift else value


def step(u, coef):
    cu, cd, cl, cr, c0 = coef
    return (
        (c0 * u + cu * rolled(u, 1, 0))
        + (cd * rolled(u, -1, 0) + cl * rolled(u, 1, 1))
        + cr * rolled(u, -1, 1)
    )


def kernel(
    tcount, scount, chunks, depth, height, width,
    guess, forcing, initial, crow, ccol, diff, out,
    prev, own, frc, raw, pks, pkr, coef, ein, eout, res, ost,
    ldsem, psend, precv, isend, ksend, krecv, esend, erecv, osem,
):
    t = lax.axis_index("tm")
    s = lax.axis_index("space")
    span = width // chunks
    total = height + 2 * TILE
    placed, _ = packing(depth)
    mid = slice(TILE, TILE + height)
    up_ok, down_ok = s > 0, s < scount - 1
    first, not_first, not_last = t == 0, t > 0, t < tcount - 1

    def cols(c):
        return pl.ds(pl.multiple_of(c * span, LANES), span)

    def window(load, c):
        left = pl.ds(pl.multiple_of(lax.rem(c * span + width - LANES, width), LANES), LANES)
        right = pl.ds(pl.multiple_of(lax.rem((c + 1) * span, width), LANES), LANES)
        return jnp.concatenate([load(left), load(cols(c)), load(right)], axis=1)

    def remote(src, dst, ssem, rsem, dt, ds):
        return pltpu.make_async_remote_copy(
            src_ref=src, dst_ref=dst, send_sem=ssem, recv_sem=rsem,
            device_id=(t + dt, s + ds), device_id_type=MESH,
        )

    loads = [pltpu.make_async_copy(guess.at[depth - 1], own, ldsem.at[0])]
    for j in range(depth):
        loads.append(pltpu.make_async_copy(forcing.at[j], frc.at[j, mid], ldsem.at[1 + j]))
    for j, ref in enumerate((crow, ccol, diff)):
        loads.append(pltpu.make_async_copy(ref, raw.at[j], ldsem.at[1 + depth + j]))
    init_load = pltpu.make_async_copy(initial, prev.at[mid], ldsem.at[4 + depth])
    for load in loads:
        load.start()
    pl.when(first)(init_load.start)

    barrier = pltpu.get_barrier_semaphore()
    count = 0
    for dt in (-1, 0, 1):
        for ds in (-1, 0, 1):
            if dt == 0 and ds == 0:
                continue
            ok = (t + dt >= 0) & (t + dt < tcount) & (s + ds >= 0) & (s + ds < scount)

            @pl.when(ok)
            def _(dt=dt, ds=ds):
                pl.semaphore_signal(barrier, inc=1, device_id=(t + dt, s + ds), device_id_type=MESH)

            count = count + ok.astype(jnp.int32)

    @pl.when(s == 0)
    def _():
        prev[0:TILE] = jnp.zeros((TILE, width), jnp.float32)
        ein[0:TILE] = jnp.zeros((TILE, width), jnp.float32)
        pkr[0] = jnp.zeros(pkr.shape[1:], jnp.float32)

    @pl.when(s == scount - 1)
    def _():
        prev[TILE + height:] = jnp.zeros((TILE, width), jnp.float32)
        ein[TILE + height:] = jnp.zeros((TILE, width), jnp.float32)
        pkr[1] = jnp.zeros(pkr.shape[1:], jnp.float32)

    @pl.when(first)
    def _():
        ein[...] = jnp.zeros((total, width), jnp.float32)

    for load in loads:
        load.wait()
    pl.when(first)(init_load.wait)
    pl.semaphore_wait(barrier, count)

    top_rows, bottom_rows = slice(0, TILE), slice(height - TILE, height)
    top_halo, bottom_halo = slice(0, TILE), slice(TILE + height, total)

    def prev_copies(c):
        last = guess.at[depth - 1]
        return (
            (not_last, remote(last.at[:, cols(c)], prev.at[mid, cols(c)],
                              psend.at[0, c], precv.at[0, c], 1, 0)),
            (not_last & down_ok, remote(last.at[bottom_rows, cols(c)], prev.at[top_halo, cols(c)],
                                        psend.at[1, c], precv.at[1, c], 1, 1)),
            (not_last & up_ok, remote(last.at[top_rows, cols(c)], prev.at[bottom_halo, cols(c)],
                                      psend.at[2, c], precv.at[2, c], 1, -1)),
            (first & down_ok, remote(initial.at[bottom_rows, cols(c)], prev.at[top_halo, cols(c)],
                                     isend.at[0, c], precv.at[1, c], 0, 1)),
            (first & up_ok, remote(initial.at[top_rows, cols(c)], prev.at[bottom_halo, cols(c)],
                                   isend.at[1, c], precv.at[2, c], 0, -1)),
        )

    def pack_copies(c):
        return (
            (down_ok, remote(pks.at[0, :, cols(c)], pkr.at[0, :, cols(c)],
                             ksend.at[0, c], krecv.at[0, c], 0, 1)),
            (up_ok, remote(pks.at[1, :, cols(c)], pkr.at[1, :, cols(c)],
                           ksend.at[1, c], krecv.at[1, c], 0, -1)),
        )

    def e_copies(c):
        return (
            (not_last, remote(eout.at[:, cols(c)], ein.at[mid, cols(c)],
                              esend.at[0, c], erecv.at[0, c], 1, 0)),
            (not_last & down_ok, remote(eout.at[bottom_rows, cols(c)], ein.at[top_halo, cols(c)],
                                        esend.at[1, c], erecv.at[1, c], 1, 1)),
            (not_last & up_ok, remote(eout.at[top_rows, cols(c)], ein.at[bottom_halo, cols(c)],
                                      esend.at[2, c], erecv.at[2, c], 1, -1)),
        )

    row = lax.broadcasted_iota(jnp.int32, (TILE, span), 0)

    def source_rows(source, rows, c):
        kind, j = source
        if kind == "f":
            return frc[j, slice(TILE + rows.start, TILE + rows.stop), cols(c)]
        return raw[j, rows, cols(c)]

    def send_start(i, carry):
        c = lax.rem(t - 1 + i + chunks, chunks)
        tiles = [[None, None] for _ in range(pks.shape[1] // TILE)]
        for source, rows, tile, offset in placed:
            low = rolled(source_rows(source, bottom_rows, c), -offset, 0)
            high = rolled(source_rows(source, top_rows, c), offset, 0)
            if tiles[tile][0] is None:
                tiles[tile] = [low, high]
            else:
                tiles[tile][0] = jnp.where(row < TILE - offset, low, tiles[tile][0])
                tiles[tile][1] = jnp.where(row >= offset, high, tiles[tile][1])
        for tile, (low, high) in enumerate(tiles):
            pks[0, tile * TILE:(tile + 1) * TILE, cols(c)] = low
            pks[1, tile * TILE:(tile + 1) * TILE, cols(c)] = high
        for ok, copy in pack_copies(c) + prev_copies(lax.rem(t + i, chunks))[:3] + prev_copies(c)[3:]:
            pl.when(ok)(copy.start)
        return carry

    lax.fori_loop(0, chunks, send_start, 0)

    def wait_recv(sem_row, dst):
        return pltpu.make_async_copy(dst, dst, sem_row)

    def prepare(i):
        c = lax.rem(t - 1 + i + chunks, chunks)
        pl.when(not_first)(wait_recv(precv.at[0, c], prev.at[mid, cols(c)]).wait)

        @pl.when(up_ok)
        def _():
            wait_recv(precv.at[1, c], prev.at[top_halo, cols(c)]).wait()
            wait_recv(krecv.at[0, c], pkr.at[0, :, cols(c)]).wait()

        @pl.when(down_ok)
        def _():
            wait_recv(precv.at[2, c], prev.at[bottom_halo, cols(c)]).wait()
            wait_recv(krecv.at[1, c], pkr.at[1, :, cols(c)]).wait()

        ext = [None, None, None]
        for (kind, j), rows, tile, offset in placed:
            part = slice(tile * TILE, (tile + 1) * TILE)
            top = rolled(pkr[0, part, cols(c)], offset, 0)
            bottom = rolled(pkr[1, part, cols(c)], -offset, 0)
            if kind == "f":
                frc[j, top_halo, cols(c)] = top
                frc[j, bottom_halo, cols(c)] = bottom
            else:
                ext[j] = jnp.concatenate([top, raw[j, :, cols(c)], bottom], axis=0)
        a, b, d = ext
        cu = jnp.maximum(a, 0.0) + d
        cd = d - jnp.minimum(a, 0.0)
        cl = jnp.maximum(b, 0.0) + d
        cr = d - jnp.minimum(b, 0.0)
        coef[0, :, cols(c)] = cu
        coef[1, :, cols(c)] = cd
        coef[2, :, cols(c)] = cl
        coef[3, :, cols(c)] = cr
        coef[4, :, cols(c)] = 1.0 - ((cu + cd) + (cl + cr))

    def coef_of(c):
        return [window(lambda lanes, n=n: coef[n, :, lanes], c) for n in range(5)]

    def relax(i):
        c = lax.rem(t + i, chunks)
        cs = coef_of(c)
        u = window(lambda lanes: prev[:, lanes], c)
        for j in range(depth):
            u = step(u, cs)
            if j < depth - 1:
                u = u + window(lambda lanes: frc[j, :, lanes], c)
        w = u[mid, LANES:LANES + span] + frc[depth - 1, mid, cols(c)]
        res[:, cols(c)] = w - own[:, cols(c)]

    def coarse(i):
        c = lax.rem(t + i, chunks)
        cs = coef_of(c)
        u = window(lambda lanes: ein[:, lanes], c)
        for _ in range(depth // 2):
            u = 2.0 * step(u, cs) - u
        e = u[mid, LANES:LANES + span] + res[:, cols(c)]
        eout[:, cols(c)] = e
        ost[depth - 1, :, cols(c)] = own[:, cols(c)] + e
        for ok, copy in e_copies(c):
            pl.when(ok)(copy.start)

    def out_copy(c):
        return pltpu.make_async_copy(ost.at[:, :, cols(c)], out.at[:, :, cols(c)], osem.at[c])

    def final(i):
        c = lax.rem(t + i, chunks)
        cs = coef_of(c)
        u = window(lambda lanes: prev[:, lanes] + ein[:, lanes], c)
        for j in range(depth - 1):
            u = step(u, cs) + window(lambda lanes: frc[j, :, lanes], c)
            ost[j, :, cols(c)] = u[mid, LANES:LANES + span]
        out_copy(c).start()

    def wait_e(i):
        c = lax.rem(t - 1 + i + chunks, chunks)

        @pl.when(not_first)
        def _():
            wait_recv(erecv.at[0, c], ein.at[mid, cols(c)]).wait()

        @pl.when(not_first & up_ok)
        def _():
            wait_recv(erecv.at[1, c], ein.at[top_halo, cols(c)]).wait()

        @pl.when(not_first & down_ok)
        def _():
            wait_recv(erecv.at[2, c], ein.at[bottom_halo, cols(c)]).wait()

    for i in range(3):
        prepare(i)
    relax(0)
    wait_e(0)
    wait_e(1)

    def sweep(i, carry):
        @pl.when(i + 2 < chunks)
        def _():
            wait_e(i + 2)

        coarse(i)

        @pl.when(i + 3 < chunks)
        def _():
            prepare(i + 3)

        @pl.when(i + 1 < chunks)
        def _():
            relax(i + 1)

        final(i)
        return carry

    lax.fori_loop(0, chunks, sweep, 0)

    def finish(c, carry):
        for ok, copy in prev_copies(c) + pack_copies(c) + e_copies(c):
            pl.when(ok)(copy.wait_send)
        out_copy(c).wait()
        return carry

    lax.fori_loop(0, chunks, finish, 0)


def on_device(tcount, scount, guess, forcing, initial, crow, ccol, diff):
    depth, height, width = guess.shape
    chunks = max(n for n in (4, 8) if width % (n * LANES) == 0)
    _, tiles = packing(depth)
    total = height + 2 * TILE
    f32 = jnp.float32
    dma = pltpu.SemaphoreType.DMA
    return pl.pallas_call(
        functools.partial(kernel, tcount, scount, chunks, depth, height, width),
        out_shape=jax.ShapeDtypeStruct(guess.shape, f32),
        in_specs=[pl.BlockSpec(memory_space=pl.ANY)] * 6,
        out_specs=pl.BlockSpec(memory_space=pl.ANY),
        scratch_shapes=[
            pltpu.VMEM((total, width), f32),
            pltpu.VMEM((height, width), f32),
            pltpu.VMEM((depth, total, width), f32),
            pltpu.VMEM((3, height, width), f32),
            pltpu.VMEM((2, tiles * TILE, width), f32),
            pltpu.VMEM((2, tiles * TILE, width), f32),
            pltpu.VMEM((5, total, width), f32),
            pltpu.VMEM((total, width), f32),
            pltpu.VMEM((height, width), f32),
            pltpu.VMEM((height, width), f32),
            pltpu.VMEM((depth, height, width), f32),
            dma((5 + depth,)),
            dma((3, chunks)),
            dma((3, chunks)),
            dma((2, chunks)),
            dma((2, chunks)),
            dma((2, chunks)),
            dma((3, chunks)),
            dma((3, chunks)),
            dma((chunks,)),
        ],
        compiler_params=pltpu.CompilerParams(
            collective_id=0, has_side_effects=True, vmem_limit_bytes=48 << 20
        ),
    )(guess, forcing, initial, crow, ccol, diff)


def solution(mesh):
    return jax.shard_map(
        functools.partial(on_device, mesh.shape["tm"], mesh.shape["space"]),
        mesh=mesh,
        in_specs=(
            P("tm", "space", None),
            P("tm", "space", None),
            P("space", None),
            P("space", None),
            P("space", None),
            P("space", None),
        ),
        out_specs=P("tm", "space", None),
        check_vma=False,
    )
```

time: 180 us -> 67.1 us (0.37)
  the two profiles are of different devices: /device:TPU:4 before, /device:TPU:7 now
where the time goes in v1:
time: 67.1 us; the launch traced here: 66.8 us
  Pallas kernels  61.3 us (91%)
  local copies, waits for them, and re-layouts  5.49 us (8%)
    pallas_call x1, Pallas kernels, on_device(): pl.pallas_call(functools.partial(kernel, tcount, scount, chunks, depth, h...  61.3 us
    unnamed x9, local copies, waits for them, and re-layouts  5.49 us

profile of v1, /device:TPU:7, one launch (start us, length us, event | category | flops | bytes accessed | tf_op | source)
XLA Modules:
  0.0 66.8 jit_solution(2552072824089017329)
XLA Ops:
  0.0 0.0 copy-start
  0.0 1.0 %copy-done = f32[32,4096]{1,0:T(8,128)S(1)} copy-done((f32[32,4096]{1,0:T(8,128)S(1)}, f32[32,4096]{1,0:T(8,128)}, u32[]{:S(2)}) %copy-start) | copy-done | bytes 524312
  1.0 0.0 copy-start.1
  1.0 1.0 %copy-done.1 = f32[32,4096]{1,0:T(8,128)S(1)} copy-done((f32[32,4096]{1,0:T(8,128)S(1)}, f32[32,4096]{1,0:T(8,128)}, u32[]{:S(2)}) %copy-start.1) | copy-done | bytes 524312
  2.1 0.0 copy-start.2
  2.1 1.0 %copy-done.2 = f32[32,4096]{1,0:T(8,128)S(1)} copy-done((f32[32,4096]{1,0:T(8,128)S(1)}, f32[32,4096]{1,0:T(8,128)}, u32[]{:S(2)}) %copy-start.2) | copy-done | bytes 524312
  3.1 0.0 copy-start.3
  3.1 1.0 %copy-done.3 = f32[32,4096]{1,0:T(8,128)S(1)} copy-done((f32[32,4096]{1,0:T(8,128)S(1)}, f32[32,4096]{1,0:T(8,128)}, u32[]{:S(2)}) %copy-start.3) | copy-done | bytes 524312
  4.2 61.3 %shard_map.64 = f32[4,32,4096]{2,1,0:T(8,128)S(1)} custom-call(f32[4,32,4096]{2,1,0:T(8,128)} %guess.1, f32[4,32,4096]{2,1,0:T(8,128)} %forcing.1, f32[32,4096]{1,0:T(8,128)S(1)} %copy-done, f32[32,4096]{1,0:T(8,128)S(1)} %copy-done.1, f32[32,4096]{1,0:T(8,128)S(1)} %copy-done.2, f32[32,4096]{1,0:T(8,128)S(1)} %copy-done.3), custom_call_target="tpu_custom_call" | custom-call | tf_op jit(solution)/shard_map/pallas_call | solution.py:316
  65.4 1.3 %copy.8 = f32[4,32,4096]{2,1,0:T(8,128)} copy(f32[4,32,4096]{2,1,0:T(8,128)S(1)} %shard_map.64) | data formatting | bytes 4194304
Async XLA Ops:
  0.0 1.0 %copy-start = (f32[32,4096]{1,0:T(8,128)S(1)}, f32[32,4096]{1,0:T(8,128)}, u32[]{:S(2)}) copy-start(f32[32,4096]{1,0:T(8,128)} %initial.1) | copy-start | bytes 1572868
  1.0 1.0 %copy-start.1 = (f32[32,4096]{1,0:T(8,128)S(1)}, f32[32,4096]{1,0:T(8,128)}, u32[]{:S(2)}) copy-start(f32[32,4096]{1,0:T(8,128)} %crow.1) | copy-start | bytes 1572868
  2.1 1.0 %copy-start.2 = (f32[32,4096]{1,0:T(8,128)S(1)}, f32[32,4096]{1,0:T(8,128)}, u32[]{:S(2)}) copy-start(f32[32,4096]{1,0:T(8,128)} %ccol.1) | copy-start | bytes 1572868
  3.1 1.0 %copy-start.3 = (f32[32,4096]{1,0:T(8,128)S(1)}, f32[32,4096]{1,0:T(8,128)}, u32[]{:S(2)}) copy-start(f32[32,4096]{1,0:T(8,128)} %diff.1) | copy-start | bytes 1572868

commit v2 on v0

v2 whole, which is shorter than its diff:
```python
import functools

import jax
import jax.numpy as jnp
from jax import lax
from jax.experimental import pallas as pl
from jax.experimental.pallas import tpu as pltpu
from jax.sharding import PartitionSpec as P

SUB = 8
LANES = 128
PIECE = 2
BLOCK = 2
MESH = pl.DeviceIdType.MESH


def shifted(x):
    lane = lax.broadcasted_iota(jnp.int32, x.shape[:2] + (LANES,), 2)
    size = x.shape[2]
    left = pltpu.roll(x, 1, 2)
    edge = left[:, :, :LANES]
    edge = jnp.where(lane == 0, pltpu.roll(edge, 1, 1), edge)
    left = jnp.concatenate([edge, left[:, :, LANES:]], axis=2)
    right = pltpu.roll(x, size - 1, 2)
    edge = right[:, :, size - LANES:]
    edge = jnp.where(lane == LANES - 1, pltpu.roll(edge, SUB - 1, 1), edge)
    right = jnp.concatenate([right[:, :, : size - LANES], edge], axis=2)
    return left, right


def kernel(
    tcount, scount, depth, height, lanes, nstart,
    guess, forcing, initial, crow, ccol, diff, out,
    prev, own, frc, raw, coef, ein, eout, res, ost, wa, wb,
    ldsem, ssend, srecv, esend, erecv, osem,
):
    t = lax.axis_index("tm")
    s = lax.axis_index("space")
    base = depth
    total = height + 2 * depth
    pieces = height // (2 * PIECE)
    up_ok, down_ok = s > 0, s < scount - 1
    first, not_first, not_last = t == 0, t > 0, t < tcount - 1
    field = pl.ds(base, height)

    def remote(src, dst, ssem, rsem, dt, ds):
        return pltpu.make_async_remote_copy(
            src_ref=src, dst_ref=dst, send_sem=ssem, recv_sem=rsem,
            device_id=(t + dt, s + ds), device_id_type=MESH,
        )

    loads = [pltpu.make_async_copy(guess, own, ldsem.at[0])]
    for j in range(depth):
        loads.append(pltpu.make_async_copy(forcing.at[j], frc.at[j, field], ldsem.at[1 + j]))
    for j, ref in enumerate((crow, ccol, diff)):
        loads.append(pltpu.make_async_copy(ref, raw.at[j, field], ldsem.at[1 + depth + j]))
    init_load = pltpu.make_async_copy(initial, prev.at[field], ldsem.at[4 + depth])
    for load in loads:
        load.start()
    pl.when(first)(init_load.start)

    barrier = pltpu.get_barrier_semaphore()
    count = 0
    for dt in (-1, 0, 1):
        for ds in (-1, 0, 1):
            if dt == 0 and ds == 0:
                continue
            ok = (t + dt >= 0) & (t + dt < tcount) & (s + ds >= 0) & (s + ds < scount)

            @pl.when(ok)
            def _(dt=dt, ds=ds):
                pl.semaphore_signal(barrier, inc=1, device_id=(t + dt, s + ds), device_id_type=MESH)

            count = count + ok.astype(jnp.int32)

    def clear(rows):
        zero = jnp.zeros((rows.size, SUB, lanes), jnp.float32)
        prev[rows] = zero
        ein[rows] = zero
        for j in range(depth - 1):
            frc[j, rows] = zero
        for j in range(3):
            raw[j, rows] = zero

    @pl.when(s == 0)
    def _():
        clear(pl.ds(0, depth))

    @pl.when(s == scount - 1)
    def _():
        clear(pl.ds(base + height, depth))

    @pl.when(first)
    def _():
        def body(i, carry):
            ein[i] = jnp.zeros((SUB, lanes), jnp.float32)
            return carry

        lax.fori_loop(0, total, body, 0)

    pl.semaphore_wait(barrier, count)

    starts = []

    def add(send_ok, src, dst, dt, ds, recv_ok, slot=None):
        n = len(starts)
        starts.append((send_ok, remote(src, dst, ssend.at[n], srecv.at[n if slot is None else slot], dt, ds), recv_ok))
        return n

    def halos(send_ok, src, dst, rows, dt, recv_ok, slots=(None, None)):
        low = add(send_ok & down_ok, src.at[pl.ds(height - rows, rows)], dst.at[pl.ds(base - rows, rows)],
                  dt, 1, None if recv_ok is None else recv_ok & up_ok, slots[0])
        high = add(send_ok & up_ok, src.at[pl.ds(0, rows)], dst.at[pl.ds(base + height, rows)],
                   dt, -1, None if recv_ok is None else recv_ok & down_ok, slots[1])
        return low, high

    always = t >= 0
    slots = halos(not_last, guess, prev, depth, 1, always)
    halos(first, initial, prev, depth, 0, None, slots)
    for j, ref in enumerate((crow, ccol, diff)):
        halos(always, ref, raw.at[j], depth - 1, 0, always)
    for j in range(depth - 1):
        halos(always, forcing.at[j], frc.at[j], depth - 1 - j, 0, always)
    add(not_last, guess, prev.at[field], 1, 0, not_first)
    assert len(starts) == nstart
    for ok, copy, _ in starts:
        pl.when(ok)(copy.start)
    for load in loads:
        load.wait()
    pl.when(first)(init_load.wait)
    for _, copy, ok in starts:
        if ok is not None:
            pl.when(ok)(copy.wait_recv)

    def coefficients(i, carry):
        row = i + 1
        a, b, d = raw[0, row], raw[1, row], raw[2, row]
        cu = jnp.maximum(a, 0.0) + d
        cd = d - jnp.minimum(a, 0.0)
        cl = jnp.maximum(b, 0.0) + d
        cr = d - jnp.minimum(b, 0.0)
        coef[0, row] = cu
        coef[1, row] = cd
        coef[2, row] = cl
        coef[3, row] = cr
        coef[4, row] = 1.0 - ((cu + cd) + (cl + cr))
        return carry

    lax.fori_loop(0, height + 2 * depth - 2, coefficients, 0)

    def step(ext, row, count):
        rows = pl.ds(row, count)
        u = ext[1:-1]
        left, right = shifted(u)
        return (
            (coef[4, rows] * u + coef[0, rows] * ext[:-2])
            + (coef[1, rows] * ext[2:] + coef[2, rows] * left)
            + coef[3, rows] * right
        )

    def sweep(src, margin, finish):
        low = base - margin

        def body(i, carry):
            row = low + i * BLOCK
            finish(row, step(src[pl.ds(row - 1, BLOCK + 2)], row, BLOCK))
            return carry

        lax.fori_loop(0, (height + 2 * margin) // BLOCK, body, 0)

    def advance(src, dst, j, margin, keep=False):
        def finish(row, value):
            value = value + frc[j, pl.ds(row, BLOCK)]
            dst[pl.ds(row, BLOCK)] = value

        sweep(src, margin, finish)

    buffers = (wa, wb)
    src = prev
    for j in range(depth - 1):
        advance(src, buffers[j % 2], j, depth - 1 - j)
        src = buffers[j % 2]

    def residual(row, value):
        rows = pl.ds(row - base, BLOCK)
        res[rows] = value + frc[depth - 1, pl.ds(row, BLOCK)] - own[rows]

    sweep(src, 0, residual)

    halo = depth - 1

    def e_copies(i):
        low, high = i * PIECE, height - (i + 1) * PIECE
        copies = [
            (not_last, not_first, remote(eout.at[pl.ds(row, PIECE)], ein.at[pl.ds(base + row, PIECE)],
                                         esend.at[side, i], erecv.at[side, i], 1, 0))
            for side, row in ((0, low), (1, high))
        ]
        rows = min(halo - low, PIECE)
        if rows > 0:
            copies.append((not_last & up_ok, not_first & down_ok, remote(
                eout.at[pl.ds(low, rows)], ein.at[pl.ds(base + height + low, rows)],
                esend.at[2, i], erecv.at[2, i], 1, -1)))
            copies.append((not_last & down_ok, not_first & up_ok, remote(
                eout.at[pl.ds(height - low - rows, rows)], ein.at[pl.ds(base - low - rows, rows)],
                esend.at[3, i], erecv.at[3, i], 1, 1)))
        return copies

    def wait_e(i):
        for _, ok, copy in e_copies(i):
            pl.when(ok)(copy.wait_recv)

    def coarse(row):
        reach = depth // 2
        x = ein[pl.ds(base + row - reach, PIECE + 2 * reach)]
        for k in range(reach):
            size = x.shape[0] - 2
            x = 2.0 * step(x, base + row - reach + k + 1, size) - x[1:-1]
        rows = pl.ds(row, PIECE)
        e = x + res[rows]
        eout[rows] = e
        ost[depth - 1, rows] = own[rows] + e

    def out_copy(j):
        return pltpu.make_async_copy(ost.at[j], out.at[j], osem.at[j])

    wait_e(0)
    for i in range(pieces):
        if i + 1 < pieces:
            wait_e(i + 1)
        coarse(i * PIECE)
        coarse(height - (i + 1) * PIECE)
        for ok, _, copy in e_copies(i):
            pl.when(ok)(copy.start)
    out_copy(depth - 1).start()

    def corrected(i, carry):
        wb[i + 1] = prev[i + 1] + ein[i + 1]
        return carry

    lax.fori_loop(0, total - 2, corrected, 0)
    src = wb
    for j in range(depth - 1):
        dst = buffers[j % 2]
        margin = depth - 2 - j

        def finish(row, value, j=j, dst=dst):
            dst[pl.ds(row, BLOCK)] = value + frc[j, pl.ds(row, BLOCK)]

        sweep(src, margin, finish)

        def stage(i, carry, j=j, dst=dst):
            ost[j, i] = dst[base + i]
            return carry

        lax.fori_loop(0, height, stage, 0)
        src = dst
        out_copy(j).start()

    for ok, copy, _ in starts:
        pl.when(ok)(copy.wait_send)
    for i in range(pieces):
        for ok, _, copy in e_copies(i):
            pl.when(ok)(copy.wait_send)
    for j in range(depth):
        out_copy(j).wait()


def on_device(tcount, scount, guess, forcing, initial, crow, ccol, diff):
    depth, height, width = guess.shape
    lanes = width // SUB
    assert lanes % LANES == 0 and height % (2 * PIECE) == 0
    total = height + 2 * depth
    nstart = 2 * (2 + 3 + depth - 1) + 1
    f32 = jnp.float32
    dma = pltpu.SemaphoreType.DMA

    def rows_of(value):
        return value.reshape(value.shape[:-1] + (SUB, lanes))

    def buffer(*dims):
        return pltpu.VMEM(dims + (SUB, lanes), f32)

    states = pl.pallas_call(
        functools.partial(kernel, tcount, scount, depth, height, lanes, nstart),
        out_shape=jax.ShapeDtypeStruct((depth, height, SUB, lanes), f32),
        in_specs=[pl.BlockSpec(memory_space=pl.ANY)] * 6,
        out_specs=pl.BlockSpec(memory_space=pl.ANY),
        scratch_shapes=[
            buffer(total),
            buffer(height),
            buffer(depth, total),
            buffer(3, total),
            buffer(5, total),
            buffer(total),
            buffer(height),
            buffer(height),
            buffer(depth, height),
            buffer(total),
            buffer(total),
            dma((5 + depth,)),
            dma((nstart,)),
            dma((nstart,)),
            dma((4, height // (2 * PIECE))),
            dma((4, height // (2 * PIECE))),
            dma((depth,)),
        ],
        compiler_params=pltpu.CompilerParams(
            collective_id=0, has_side_effects=True, vmem_limit_bytes=40 << 20
        ),
    )(*map(rows_of, (guess[depth - 1], forcing, initial, crow, ccol, diff)))
    return states.reshape(guess.shape)


def solution(mesh):
    return jax.shard_map(
        functools.partial(on_device, mesh.shape["tm"], mesh.shape["space"]),
        mesh=mesh,
        in_specs=(
            P("tm", "space", None),
            P("tm", "space", None),
            P("space", None),
            P("space", None),
            P("space", None),
            P("space", None),
        ),
        out_specs=P("tm", "space", None),
        check_vma=False,
    )
```

time: 180 us -> 62.1 us (0.35)
  the two profiles are of different devices: /device:TPU:4 before, /device:TPU:7 now
where the time goes in v2:
time: 62.1 us; the launch traced here: 61.9 us
  Pallas kernels  55.6 us (90%)
  local copies, waits for them, and re-layouts  6.25 us (10%)
    pallas_call x1, Pallas kernels, on_device(): pl.pallas_call(functools.partial(kernel, tcount, scount, depth, height, l...  55.6 us
    unnamed x16, local copies, waits for them, and re-layouts  3.53 us
    reshape x1, local copies, waits for them, and re-layouts, on_device(): return states.reshape(guess.shape)  1.53 us

profile of v2, /device:TPU:7, one launch (start us, length us, event | category | flops | bytes accessed | tf_op | source)
XLA Modules:
  0.0 61.9 jit_solution(15176422005996595184)
XLA Ops:
  0.0 0.0 copy-start.2
  0.0 0.0 copy-start.1
  0.0 0.0 copy-start.3
  0.0 1.2 %slice.3 = f32[1,32,4096]{2,1,0:T(8,128)S(1)} slice(f32[4,32,4096]{2,1,0:T(8,128)} %param.6), slice={[3:4], [0:32], [0:4096]} | slice | bytes 1048576 | tf_op jit(solution)/shard_map/slice | solution.py:311
  1.2 0.0 copy-start.4
  1.2 0.3 copy.7
  1.5 0.0 copy-done.1
  1.5 0.0 copy-start
  1.6 0.3 copy.9
  1.9 0.0 copy-done.2
  1.9 0.3 copy.10
  2.2 0.0 copy-done.3
  2.2 0.3 copy.11
  2.5 0.0 copy-done.4
  2.5 0.3 copy.12
  2.9 0.3 copy-done
  3.2 1.6 %copy.8 = f32[16,8,8,512]{3,2,1,0:T(8,128)S(1)} copy(f32[16,8,8,512]{3,1,2,0:T(8,128)S(1)} %bitcast.23) | data formatting | bytes 4194304
  4.8 55.6 %shard_map.64 = f32[4,32,8,512]{3,2,1,0:T(8,128)S(1)} custom-call(f32[32,8,512]{2,1,0:T(8,128)S(1)} %bitcast.18, f32[4,32,8,512]{3,2,1,0:T(8,128)S(1)} %bitcast.17, f32[32,8,512]{2,1,0:T(8,128)S(1)} %bitcast.19, f32[32,8,512]{2,1,0:T(8,128)S(1)} %bitcast.20, f32[32,8,512]{2,1,0:T(8,128)S(1)} %bitcast.21, f32[32,8,512]{2,1,0:T(8,128)S(1)} %bitcast.22), custom_call_target="tpu_custom_call" | custom-call | tf_op jit(solution)/shard_map/pallas_call | solution.py:284
  60.4 1.5 %reshape.23 = f32[4,32,4096]{2,1,0:T(8,128)} reshape(f32[4,32,8,512]{3,2,1,0:T(8,128)S(1)} %shard_map.64) | data formatting | bytes 4194304 | tf_op jit(solution)/shard_map/reshape | solution.py:312
Async XLA Ops:
  0.0 1.9 %copy-start.2 = (f32[32,4096]{1,0:T(8,128)S(1)}, f32[32,4096]{1,0:T(8,128)}, u32[]{:S(2)}) copy-start(f32[32,4096]{1,0:T(8,128)} %param.9) | copy-start | bytes 1572868
  0.0 1.5 %copy-start.1 = (f32[32,4096]{1,0:T(8,128)S(1)}, f32[32,4096]{1,0:T(8,128)}, u32[]{:S(2)}) copy-start(f32[32,4096]{1,0:T(8,128)} %param.8) | copy-start | bytes 1572868
  0.0 2.2 %copy-start.3 = (f32[32,4096]{1,0:T(8,128)S(1)}, f32[32,4096]{1,0:T(8,128)}, u32[]{:S(2)}) copy-start(f32[32,4096]{1,0:T(8,128)} %param.10) | copy-start | bytes 1572868
  1.2 1.3 %copy-start.4 = (f32[32,4096]{1,0:T(8,128)S(1)}, f32[32,4096]{1,0:T(8,128)}, u32[]{:S(2)}) copy-start(f32[32,4096]{1,0:T(8,128)} %param.11) | copy-start | bytes 1572868
  1.5 1.6 %copy-start = (f32[4,32,4096]{2,1,0:T(8,128)S(1)}, f32[4,32,4096]{2,1,0:T(8,128)}, u32[]{:S(2)}) copy-start(f32[4,32,4096]{2,1,0:T(8,128)} %param.7) | copy-start | bytes 6291460

commit v3 on v2

--- a/solution.py
+++ b/solution.py
@@ -10,6 +10,7 @@
 SUB = 8
 LANES = 128
 PIECE = 2
+FLIGHT = 2
 BLOCK = 2
 MESH = pl.DeviceIdType.MESH
 
@@ -31,8 +32,8 @@
 def kernel(
     tcount, scount, depth, height, lanes, nstart,
     guess, forcing, initial, crow, ccol, diff, out,
-    prev, own, frc, raw, coef, ein, eout, res, ost, wa, wb,
-    ldsem, ssend, srecv, esend, erecv, osem,
+    prev, frc, raw, coef, ein, eout, res, wa, wb,
+    ssend, srecv, esend, erecv,
 ):
     t = lax.axis_index("tm")
     s = lax.axis_index("space")
@@ -48,16 +49,6 @@
             src_ref=src, dst_ref=dst, send_sem=ssem, recv_sem=rsem,
             device_id=(t + dt, s + ds), device_id_type=MESH,
         )
-
-    loads = [pltpu.make_async_copy(guess, own, ldsem.at[0])]
-    for j in range(depth):
-        loads.append(pltpu.make_async_copy(forcing.at[j], frc.at[j, field], ldsem.at[1 + j]))
-    for j, ref in enumerate((crow, ccol, diff)):
-        loads.append(pltpu.make_async_copy(ref, raw.at[j, field], ldsem.at[1 + depth + j]))
-    init_load = pltpu.make_async_copy(initial, prev.at[field], ldsem.at[4 + depth])
-    for load in loads:
-        load.start()
-    pl.when(first)(init_load.start)
 
     barrier = pltpu.get_barrier_semaphore()
     count = 0
@@ -125,16 +116,7 @@
     assert len(starts) == nstart
     for ok, copy, _ in starts:
         pl.when(ok)(copy.start)
-    for load in loads:
-        load.wait()
-    pl.when(first)(init_load.wait)
-    for _, copy, ok in starts:
-        if ok is not None:
-            pl.when(ok)(copy.wait_recv)
-
-    def coefficients(i, carry):
-        row = i + 1
-        a, b, d = raw[0, row], raw[1, row], raw[2, row]
+    def coefficients(row, a, b, d):
         cu = jnp.maximum(a, 0.0) + d
         cd = d - jnp.minimum(a, 0.0)
         cl = jnp.maximum(b, 0.0) + d
@@ -144,9 +126,30 @@
         coef[2, row] = cl
         coef[3, row] = cr
         coef[4, row] = 1.0 - ((cu + cd) + (cl + cr))
+
+    def local(i, carry):
+        coefficients(base + i, crow[i], ccol[i], diff[i])
+        for j in range(depth - 1):
+            frc[j, base + i] = forcing[j, i]
         return carry
 
-    lax.fori_loop(0, height + 2 * depth - 2, coefficients, 0)
+    lax.fori_loop(0, height, local, 0)
+
+    @pl.when(first)
+    def _():
+        def body(i, carry):
+            prev[base + i] = initial[i]
+            return carry
+
+        lax.fori_loop(0, height, body, 0)
+
+    for _, copy, ok in starts:
+        if ok is not None:
+            pl.when(ok)(copy.wait_recv)
+
+    edges = list(range(1, base)) + list(range(base + height, total - 1))
+    for row in edges:
+        coefficients(row, raw[0, row], raw[1, row], raw[2, row])
 
     def step(ext, row, count):
         rows = pl.ds(row, count)
@@ -183,7 +186,7 @@
 
     def residual(row, value):
         rows = pl.ds(row - base, BLOCK)
-        res[rows] = value + frc[depth - 1, pl.ds(row, BLOCK)] - own[rows]
+        res[rows] = value + forcing[depth - 1, rows] - guess[rows]
 
     sweep(src, 0, residual)
 
@@ -219,10 +222,7 @@
         rows = pl.ds(row, PIECE)
         e = x + res[rows]
         eout[rows] = e
-        ost[depth - 1, rows] = own[rows] + e
-
-    def out_copy(j):
-        return pltpu.make_async_copy(ost.at[j], out.at[j], osem.at[j])
+        out[depth - 1, rows] = guess[rows] + e
 
     wait_e(0)
     for i in range(pieces):
@@ -230,9 +230,11 @@
             wait_e(i + 1)
         coarse(i * PIECE)
         coarse(height - (i + 1) * PIECE)
+        if i >= FLIGHT:
+            for ok, _, copy in e_copies(i - FLIGHT):
+                pl.when(ok)(copy.wait_send)
         for ok, _, copy in e_copies(i):
             pl.when(ok)(copy.start)
-    out_copy(depth - 1).start()
 
     def corrected(i, carry):
         wb[i + 1] = prev[i + 1] + ein[i + 1]
@@ -245,25 +247,23 @@
         margin = depth - 2 - j
 
         def finish(row, value, j=j, dst=dst):
-            dst[pl.ds(row, BLOCK)] = value + frc[j, pl.ds(row, BLOCK)]
-
-        sweep(src, margin, finish)
-
-        def stage(i, carry, j=j, dst=dst):
-            ost[j, i] = dst[base + i]
-            return carry
-
-        lax.fori_loop(0, height, stage, 0)
+            value = value + frc[j, pl.ds(row, BLOCK)]
+            out[j, pl.ds(row - base, BLOCK)] = value
+            if j < depth - 2:
+                dst[pl.ds(row, BLOCK)] = value
+
+        sweep(src, 0, finish)
+        if margin:
+            for row in (base - margin, base + height):
+                rows = pl.ds(row, margin)
+                dst[rows] = step(src[pl.ds(row - 1, margin + 2)], row, margin) + frc[j, rows]
         src = dst
-        out_copy(j).start()
 
     for ok, copy, _ in starts:
         pl.when(ok)(copy.wait_send)
-    for i in range(pieces):
+    for i in range(max(0, pieces - FLIGHT), pieces):
         for ok, _, copy in e_copies(i):
             pl.when(ok)(copy.wait_send)
-    for j in range(depth):
-        out_copy(j).wait()
 
 
 def on_device(tcount, scount, guess, forcing, initial, crow, ccol, diff):
@@ -284,26 +284,22 @@
     states = pl.pallas_call(
         functools.partial(kernel, tcount, scount, depth, height, lanes, nstart),
         out_shape=jax.ShapeDtypeStruct((depth, height, SUB, lanes), f32),
-        in_specs=[pl.BlockSpec(memory_space=pl.ANY)] * 6,
-        out_specs=pl.BlockSpec(memory_space=pl.ANY),
+        in_specs=[pl.BlockSpec(memory_space=pltpu.VMEM)] * 6,
+        out_specs=pl.BlockSpec(memory_space=pltpu.VMEM),
         scratch_shapes=[
             buffer(total),
-            buffer(height),
-            buffer(depth, total),
+            buffer(depth - 1, total),
             buffer(3, total),
             buffer(5, total),
             buffer(total),
             buffer(height),
             buffer(height),
-            buffer(depth, height),
             buffer(total),
             buffer(total),
-            dma((5 + depth,)),
             dma((nstart,)),
             dma((nstart,)),
             dma((4, height // (2 * PIECE))),
             dma((4, height // (2 * PIECE))),
-            dma((depth,)),
         ],
         compiler_params=pltpu.CompilerParams(
             collective_id=0, has_side_effects=True, vmem_limit_bytes=40 << 20

time: 62.1 us -> 60.5 us (0.974)
  Pallas kernels: 55.6 us -> 54 us
    pallas_call x1, Pallas kernels: 55.6 us -> 54 us  [on_device(): pl.pallas_call(functools.partial(kernel, tcount, scount, depth, height, l...]
where the time goes in v3:
time: 60.5 us; the launch traced here: 60.4 us
  Pallas kernels  54 us (89%)
  local copies, waits for them, and re-layouts  6.25 us (10%)
    pallas_call x1, Pallas kernels, on_device(): pl.pallas_call(functools.partial(kernel, tcount, scount, depth, height, l...  54 us
    unnamed x16, local copies, waits for them, and re-layouts  3.53 us
    reshape x1, local copies, waits for them, and re-layouts, on_device(): return states.reshape(guess.shape)  1.53 us

profile of v3, /device:TPU:7, one launch (start us, length us, event | category | flops | bytes accessed | tf_op | source)
XLA Modules:
  0.0 60.4 jit_solution(1321124211908761254)
XLA Ops:
  0.0 0.0 copy-start.2
  0.0 0.0 copy-start.1
  0.0 0.0 copy-start.3
  0.0 1.2 %slice.3 = f32[1,32,4096]{2,1,0:T(8,128)S(1)} slice(f32[4,32,4096]{2,1,0:T(8,128)} %param.6), slice={[3:4], [0:32], [0:4096]} | slice | bytes 1048576 | tf_op jit(solution)/shard_map/slice | solution.py:307
  1.2 0.0 copy-start.4
  1.2 0.3 copy.7
  1.5 0.0 copy-done.1
  1.5 0.0 copy-start
  1.6 0.3 copy.9
  1.9 0.0 copy-done.2
  1.9 0.3 copy.10
  2.2 0.0 copy-done.3
  2.2 0.3 copy.11
  2.5 0.0 copy-done.4
  2.5 0.3 copy.12
  2.9 0.3 copy-done
  3.2 1.6 %copy.8 = f32[16,8,8,512]{3,2,1,0:T(8,128)S(1)} copy(f32[16,8,8,512]{3,1,2,0:T(8,128)S(1)} %bitcast.23) | data formatting | bytes 4194304
  4.8 54.0 %shard_map.64 = f32[4,32,8,512]{3,2,1,0:T(8,128)S(1)} custom-call(f32[32,8,512]{2,1,0:T(8,128)S(1)} %bitcast.18, f32[4,32,8,512]{3,2,1,0:T(8,128)S(1)} %bitcast.17, f32[32,8,512]{2,1,0:T(8,128)S(1)} %bitcast.19, f32[32,8,512]{2,1,0:T(8,128)S(1)} %bitcast.20, f32[32,8,512]{2,1,0:T(8,128)S(1)} %bitcast.21, f32[32,8,512]{2,1,0:T(8,128)S(1)} %bitcast.22), custom_call_target="tpu_custom_call" | custom-call | tf_op jit(solution)/shard_map/pallas_call | solution.py:284
  58.8 1.5 %reshape.23 = f32[4,32,4096]{2,1,0:T(8,128)} reshape(f32[4,32,8,512]{3,2,1,0:T(8,128)S(1)} %shard_map.64) | data formatting | bytes 4194304 | tf_op jit(solution)/shard_map/reshape | solution.py:308
Async XLA Ops:
  0.0 1.9 %copy-start.2 = (f32[32,4096]{1,0:T(8,128)S(1)}, f32[32,4096]{1,0:T(8,128)}, u32[]{:S(2)}) copy-start(f32[32,4096]{1,0:T(8,128)} %param.9) | copy-start | bytes 1572868
  0.0 1.5 %copy-start.1 = (f32[32,4096]{1,0:T(8,128)S(1)}, f32[32,4096]{1,0:T(8,128)}, u32[]{:S(2)}) copy-start(f32[32,4096]{1,0:T(8,128)} %param.8) | copy-start | bytes 1572868
  0.0 2.2 %copy-start.3 = (f32[32,4096]{1,0:T(8,128)S(1)}, f32[32,4096]{1,0:T(8,128)}, u32[]{:S(2)}) copy-start(f32[32,4096]{1,0:T(8,128)} %param.10) | copy-start | bytes 1572868
  1.2 1.3 %copy-start.4 = (f32[32,4096]{1,0:T(8,128)S(1)}, f32[32,4096]{1,0:T(8,128)}, u32[]{:S(2)}) copy-start(f32[32,4096]{1,0:T(8,128)} %param.11) | copy-start | bytes 1572868
  1.5 1.6 %copy-start = (f32[4,32,4096]{2,1,0:T(8,128)S(1)}, f32[4,32,4096]{2,1,0:T(8,128)}, u32[]{:S(2)}) copy-start(f32[4,32,4096]{2,1,0:T(8,128)} %param.7) | copy-start | bytes 6291460

commit v4 on v3

--- a/solution.py
+++ b/solution.py
@@ -11,7 +11,7 @@
 LANES = 128
 PIECE = 2
 FLIGHT = 2
-BLOCK = 2
+BLOCK = 8
 MESH = pl.DeviceIdType.MESH
 
 
@@ -32,9 +32,10 @@
 def kernel(
     tcount, scount, depth, height, lanes, nstart,
     guess, forcing, initial, crow, ccol, diff, out,
-    prev, frc, raw, coef, ein, eout, res, wa, wb,
-    ssend, srecv, esend, erecv,
+    prev, frc, raw, coef, ein, eout, res, *rest,
 ):
+    levels = tuple(rest[: depth - 1])
+    ssend, srecv, esend, erecv = rest[depth - 1:]
     t = lax.axis_index("tm")
     s = lax.axis_index("space")
     base = depth
@@ -143,13 +144,7 @@
 
         lax.fori_loop(0, height, body, 0)
 
-    for _, copy, ok in starts:
-        if ok is not None:
-            pl.when(ok)(copy.wait_recv)
-
-    edges = list(range(1, base)) + list(range(base + height, total - 1))
-    for row in edges:
-        coefficients(row, raw[0, row], raw[1, row], raw[2, row])
+    pl.when(not_first)(starts[-1][1].wait_recv)
 
     def step(ext, row, count):
         rows = pl.ds(row, count)
@@ -161,34 +156,38 @@
             + coef[3, rows] * right
         )
 
-    def sweep(src, margin, finish):
-        low = base - margin
-
+    def sweep(src, low, high, finish):
         def body(i, carry):
-            row = low + i * BLOCK
-            finish(row, step(src[pl.ds(row - 1, BLOCK + 2)], row, BLOCK))
+            row = jnp.minimum(low + i * BLOCK, high - BLOCK)
+            finish(row, step(src[pl.ds(row - 1, BLOCK + 2)], row, BLOCK), BLOCK)
             return carry
 
-        lax.fori_loop(0, (height + 2 * margin) // BLOCK, body, 0)
-
-    def advance(src, dst, j, margin, keep=False):
-        def finish(row, value):
-            value = value + frc[j, pl.ds(row, BLOCK)]
-            dst[pl.ds(row, BLOCK)] = value
-
-        sweep(src, margin, finish)
-
-    buffers = (wa, wb)
-    src = prev
-    for j in range(depth - 1):
-        advance(src, buffers[j % 2], j, depth - 1 - j)
-        src = buffers[j % 2]
-
-    def residual(row, value):
-        rows = pl.ds(row - base, BLOCK)
-        res[rows] = value + forcing[depth - 1, rows] - guess[rows]
-
-    sweep(src, 0, residual)
+        lax.fori_loop(0, -(-(high - low) // BLOCK), body, 0)
+
+    fields = (prev,) + levels
+
+    def relaxed(j):
+        def finish(row, value, size):
+            if j < depth - 1:
+                rows = pl.ds(row, size)
+                levels[j][rows] = value + frc[j, rows]
+            else:
+                rows = pl.ds(row - base, size)
+                res[rows] = value + forcing[j, rows] - guess[rows]
+
+        return finish
+
+    for j in range(depth):
+        sweep(fields[j], base + j + 1, base + height - j - 1, relaxed(j))
+    for _, copy, ok in starts[:-1]:
+        if ok is not None:
+            pl.when(ok)(copy.wait_recv)
+    edges = list(range(1, base)) + list(range(base + height, total - 1))
+    for row in edges:
+        coefficients(row, raw[0, row], raw[1, row], raw[2, row])
+    for j in range(depth):
+        for row in (base - depth + 1 + j, base + height - j - 1):
+            relaxed(j)(row, step(fields[j][pl.ds(row - 1, depth + 2)], row, depth), depth)
 
     halo = depth - 1
 
@@ -237,22 +236,23 @@
             pl.when(ok)(copy.start)
 
     def corrected(i, carry):
-        wb[i + 1] = prev[i + 1] + ein[i + 1]
+        levels[-1][i + 1] = prev[i + 1] + ein[i + 1]
         return carry
 
     lax.fori_loop(0, total - 2, corrected, 0)
-    src = wb
+    src = levels[-1]
     for j in range(depth - 1):
-        dst = buffers[j % 2]
+        dst = levels[j % 2]
         margin = depth - 2 - j
 
-        def finish(row, value, j=j, dst=dst):
-            value = value + frc[j, pl.ds(row, BLOCK)]
-            out[j, pl.ds(row - base, BLOCK)] = value
+        def finish(row, value, size, j=j, dst=dst):
+            rows = pl.ds(row, size)
+            value = value + frc[j, rows]
+            out[j, pl.ds(row - base, size)] = value
             if j < depth - 2:
-                dst[pl.ds(row, BLOCK)] = value
-
-        sweep(src, 0, finish)
+                dst[rows] = value
+
+        sweep(src, base, base + height, finish)
         if margin:
             for row in (base - margin, base + height):
                 rows = pl.ds(row, margin)
@@ -294,8 +294,7 @@
             buffer(total),
             buffer(height),
             buffer(height),
-            buffer(total),
-            buffer(total),
+            *[buffer(total) for _ in range(depth - 1)],
             dma((nstart,)),
             dma((nstart,)),
             dma((4, height // (2 * PIECE))),

time: 60.5 us -> 52.1 us (0.86)
  Pallas kernels: 54 us -> 45.6 us
    pallas_call x1, Pallas kernels: 54 us -> 45.6 us  [on_device(): pl.pallas_call(functools.partial(kernel, tcount, scount, depth, height, l...]
where the time goes in v4:
time: 52.1 us; the launch traced here: 51.9 us
  Pallas kernels  45.6 us (88%)
  local copies, waits for them, and re-layouts  6.25 us (12%)
    pallas_call x1, Pallas kernels, on_device(): pl.pallas_call(functools.partial(kernel, tcount, scount, depth, height, l...  45.6 us
    unnamed x16, local copies, waits for them, and re-layouts  3.53 us
    reshape x1, local copies, waits for them, and re-layouts, on_device(): return states.reshape(guess.shape)  1.53 us
    slice x1, local copies, waits for them, and re-layouts, on_device(): guess[depth - 1]  1.2 us

profile of v4, /device:TPU:7, one launch (start us, length us, event | category | flops | bytes accessed | tf_op | source)
XLA Modules:
  0.0 51.9 jit_solution(9289877971231878653)
XLA Ops:
  0.0 0.0 copy-start.2
  0.0 0.0 copy-start.1
  0.0 0.0 copy-start.3
  0.0 1.2 %slice.3 = f32[1,32,4096]{2,1,0:T(8,128)S(1)} slice(f32[4,32,4096]{2,1,0:T(8,128)} %param.6), slice={[3:4], [0:32], [0:4096]} | slice | bytes 1048576 | tf_op jit(solution)/shard_map/slice | solution.py:306
  1.2 0.0 copy-start.4
  1.2 0.3 copy.7
  1.5 0.0 copy-done.1
  1.5 0.0 copy-start
  1.6 0.3 copy.9
  1.9 0.0 copy-done.2
  1.9 0.3 copy.10
  2.2 0.0 copy-done.3
  2.2 0.3 copy.11
  2.5 0.0 copy-done.4
  2.5 0.3 copy.12
  2.9 0.3 copy-done
  3.2 1.6 %copy.8 = f32[16,8,8,512]{3,2,1,0:T(8,128)S(1)} copy(f32[16,8,8,512]{3,1,2,0:T(8,128)S(1)} %bitcast.23) | data formatting | bytes 4194304
  4.8 45.6 %shard_map.64 = f32[4,32,8,512]{3,2,1,0:T(8,128)S(1)} custom-call(f32[32,8,512]{2,1,0:T(8,128)S(1)} %bitcast.18, f32[4,32,8,512]{3,2,1,0:T(8,128)S(1)} %bitcast.17, f32[32,8,512]{2,1,0:T(8,128)S(1)} %bitcast.19, f32[32,8,512]{2,1,0:T(8,128)S(1)} %bitcast.20, f32[32,8,512]{2,1,0:T(8,128)S(1)} %bitcast.21, f32[32,8,512]{2,1,0:T(8,128)S(1)} %bitcast.22), custom_call_target="tpu_custom_call" | custom-call | tf_op jit(solution)/shard_map/pallas_call | solution.py:284
  50.4 1.5 %reshape.23 = f32[4,32,4096]{2,1,0:T(8,128)} reshape(f32[4,32,8,512]{3,2,1,0:T(8,128)S(1)} %shard_map.64) | data formatting | bytes 4194304 | tf_op jit(solution)/shard_map/reshape | solution.py:307
Async XLA Ops:
  0.0 1.9 %copy-start.2 = (f32[32,4096]{1,0:T(8,128)S(1)}, f32[32,4096]{1,0:T(8,128)}, u32[]{:S(2)}) copy-start(f32[32,4096]{1,0:T(8,128)} %param.9) | copy-start | bytes 1572868
  0.0 1.5 %copy-start.1 = (f32[32,4096]{1,0:T(8,128)S(1)}, f32[32,4096]{1,0:T(8,128)}, u32[]{:S(2)}) copy-start(f32[32,4096]{1,0:T(8,128)} %param.8) | copy-start | bytes 1572868
  0.0 2.2 %copy-start.3 = (f32[32,4096]{1,0:T(8,128)S(1)}, f32[32,4096]{1,0:T(8,128)}, u32[]{:S(2)}) copy-start(f32[32,4096]{1,0:T(8,128)} %param.10) | copy-start | bytes 1572868
  1.2 1.3 %copy-start.4 = (f32[32,4096]{1,0:T(8,128)S(1)}, f32[32,4096]{1,0:T(8,128)}, u32[]{:S(2)}) copy-start(f32[32,4096]{1,0:T(8,128)} %param.11) | copy-start | bytes 1572868
  1.5 1.6 %copy-start = (f32[4,32,4096]{2,1,0:T(8,128)S(1)}, f32[4,32,4096]{2,1,0:T(8,128)}, u32[]{:S(2)}) copy-start(f32[4,32,4096]{2,1,0:T(8,128)} %param.7) | copy-start | bytes 6291460

commit v5 on v4

--- a/solution.py
+++ b/solution.py
@@ -115,7 +115,7 @@
         halos(always, forcing.at[j], frc.at[j], depth - 1 - j, 0, always)
     add(not_last, guess, prev.at[field], 1, 0, not_first)
     assert len(starts) == nstart
-    for ok, copy, _ in starts:
+    for ok, copy, _ in starts[-1:] + starts[2:-1] + starts[:2]:
         pl.when(ok)(copy.start)
     def coefficients(row, a, b, d):
         cu = jnp.maximum(a, 0.0) + d
@@ -206,7 +206,7 @@
             copies.append((not_last & down_ok, not_first & up_ok, remote(
                 eout.at[pl.ds(height - low - rows, rows)], ein.at[pl.ds(base - low - rows, rows)],
                 esend.at[3, i], erecv.at[3, i], 1, 1)))
-        return copies
+        return copies[2:] + copies[:2]
 
     def wait_e(i):
         for _, ok, copy in e_copies(i):
@@ -223,10 +223,12 @@
         eout[rows] = e
         out[depth - 1, rows] = guess[rows] + e
 
-    wait_e(0)
+    ahead = -(-(depth // 2) // PIECE)
+    for i in range(ahead):
+        wait_e(i)
     for i in range(pieces):
-        if i + 1 < pieces:
-            wait_e(i + 1)
+        if i + ahead < pieces:
+            wait_e(i + ahead)
         coarse(i * PIECE)
         coarse(height - (i + 1) * PIECE)
         if i >= FLIGHT:

time: 52.1 us -> 51 us (0.979)
  Pallas kernels: 45.6 us -> 44.5 us
    pallas_call x1, Pallas kernels: 45.6 us -> 44.5 us  [on_device(): pl.pallas_call(functools.partial(kernel, tcount, scount, depth, height, l...]
where the time goes in v5:
time: 51 us; the launch traced here: 50.9 us
  Pallas kernels  44.5 us (87%)
  local copies, waits for them, and re-layouts  6.25 us (12%)
    pallas_call x1, Pallas kernels, on_device(): pl.pallas_call(functools.partial(kernel, tcount, scount, depth, height, l...  44.5 us
    unnamed x16, local copies, waits for them, and re-layouts  3.53 us
    reshape x1, local copies, waits for them, and re-layouts, on_device(): return states.reshape(guess.shape)  1.53 us
    slice x1, local copies, waits for them, and re-layouts, on_device(): guess[depth - 1]  1.2 us

profile of v5, /device:TPU:7, one launch (start us, length us, event | category | flops | bytes accessed | tf_op | source)
XLA Modules:
  0.0 50.9 jit_solution(10024125667203143991)
XLA Ops:
  0.0 0.0 copy-start.2
  0.0 0.0 copy-start.1
  0.0 0.0 copy-start.3
  0.0 1.2 %slice.3 = f32[1,32,4096]{2,1,0:T(8,128)S(1)} slice(f32[4,32,4096]{2,1,0:T(8,128)} %param.6), slice={[3:4], [0:32], [0:4096]} | slice | bytes 1048576 | tf_op jit(solution)/shard_map/slice | solution.py:308
  1.2 0.0 copy-start.4
  1.2 0.3 copy.7
  1.5 0.0 copy-done.1
  1.5 0.0 copy-start
  1.6 0.3 copy.9
  1.9 0.0 copy-done.2
  1.9 0.3 copy.10
  2.2 0.0 copy-done.3
  2.2 0.3 copy.11
  2.5 0.0 copy-done.4
  2.5 0.3 copy.12
  2.9 0.3 copy-done
  3.2 1.6 %copy.8 = f32[16,8,8,512]{3,2,1,0:T(8,128)S(1)} copy(f32[16,8,8,512]{3,1,2,0:T(8,128)S(1)} %bitcast.23) | data formatting | bytes 4194304
  4.8 44.5 %shard_map.64 = f32[4,32,8,512]{3,2,1,0:T(8,128)S(1)} custom-call(f32[32,8,512]{2,1,0:T(8,128)S(1)} %bitcast.18, f32[4,32,8,512]{3,2,1,0:T(8,128)S(1)} %bitcast.17, f32[32,8,512]{2,1,0:T(8,128)S(1)} %bitcast.19, f32[32,8,512]{2,1,0:T(8,128)S(1)} %bitcast.20, f32[32,8,512]{2,1,0:T(8,128)S(1)} %bitcast.21, f32[32,8,512]{2,1,0:T(8,128)S(1)} %bitcast.22), custom_call_target="tpu_custom_call" | custom-call | tf_op jit(solution)/shard_map/pallas_call | solution.py:286
  49.3 1.5 %reshape.23 = f32[4,32,4096]{2,1,0:T(8,128)} reshape(f32[4,32,8,512]{3,2,1,0:T(8,128)S(1)} %shard_map.64) | data formatting | bytes 4194304 | tf_op jit(solution)/shard_map/reshape | solution.py:309
Async XLA Ops:
  0.0 1.9 %copy-start.2 = (f32[32,4096]{1,0:T(8,128)S(1)}, f32[32,4096]{1,0:T(8,128)}, u32[]{:S(2)}) copy-start(f32[32,4096]{1,0:T(8,128)} %param.9) | copy-start | bytes 1572868
  0.0 1.5 %copy-start.1 = (f32[32,4096]{1,0:T(8,128)S(1)}, f32[32,4096]{1,0:T(8,128)}, u32[]{:S(2)}) copy-start(f32[32,4096]{1,0:T(8,128)} %param.8) | copy-start | bytes 1572868
  0.0 2.2 %copy-start.3 = (f32[32,4096]{1,0:T(8,128)S(1)}, f32[32,4096]{1,0:T(8,128)}, u32[]{:S(2)}) copy-start(f32[32,4096]{1,0:T(8,128)} %param.10) | copy-start | bytes 1572868
  1.2 1.3 %copy-start.4 = (f32[32,4096]{1,0:T(8,128)S(1)}, f32[32,4096]{1,0:T(8,128)}, u32[]{:S(2)}) copy-start(f32[32,4096]{1,0:T(8,128)} %param.11) | copy-start | bytes 1572868
  1.5 1.6 %copy-start = (f32[4,32,4096]{2,1,0:T(8,128)S(1)}, f32[4,32,4096]{2,1,0:T(8,128)}, u32[]{:S(2)}) copy-start(f32[4,32,4096]{2,1,0:T(8,128)} %param.7) | copy-start | bytes 6291460
